TPU v7x, 32 devices: a whole 2x2x4 slice. The times are simulated.
32 devices in a mesh: rep: 8 (over y, x, core), shard: 4 (over z).
Axes of the slice: x: 2, y: 2, z: 4, core: 2. Of those that a mesh axis runs over, the one named last changes fastest.
Arguments:
- tokens: bfloat16 [16, 1024, 768], P('rep', 'shard'), may hold values from -6 to 6
- gain_attn: bfloat16 [768], P('shard'), may hold values from 0.25 to 1.75
- bias_attn: bfloat16 [768], P('shard'), may hold values from -1.5 to 1.5
- w_qkv: bfloat16 [768, 2304], P('shard'), may hold values from -0.21875 to 0.21875
- w_feature: bfloat16 [768, 128], P('shard'), may hold values from -1.5 to 1.5
- w_out: bfloat16 [768, 768], P('shard'), may hold values from -0.875 to 0.875
- gain_mlp: bfloat16 [768], P('shard'), may hold values from 0.25 to 1.75
- bias_mlp: bfloat16 [768], P('shard'), may hold values from -1.5 to 1.5
- w_up: bfloat16 [768, 3072], P('shard'), may hold values from -0.21875 to 0.21875
- w_down: bfloat16 [3072, 768], P('shard'), may hold values from -0.109375 to 0.109375
- cotangent: bfloat16 [16, 1024, 768], P('rep', 'shard'), may hold values from -6 to 6
Outputs:
- block_out: bfloat16 [16, 1024, 768], P('rep', 'shard')
- grad_tokens: bfloat16 [16, 1024, 768], P('rep', 'shard')
- grad_gain_attn: float32 [768], P('shard')
- grad_bias_attn: float32 [768], P('shard')
- grad_w_qkv: float32 [768, 2304], P('shard')
- grad_w_feature: float32 [768, 128], P('shard')
- grad_w_out: float32 [768, 768], P('shard')
- grad_gain_mlp: float32 [768], P('shard')
- grad_bias_mlp: float32 [768], P('shard')
- grad_w_up: float32 [768, 3072], P('shard')
- grad_w_down: float32 [3072, 768], P('shard')
All inputs are finite; a program needn't handle non-finite values.
Results may differ from a plain program's by a relative error of at most 0.019.
Values may be sent and summed in bfloat16 or wider, within the bound.
No kernel may reach another device: no remote copies, remote signals or barrier semaphores. Data moves between devices by JAX's collectives and lax.ppermute only.
A program may use at most 192 MiB of HBM per device.

v0:
```python
import jax
import jax.numpy as jnp
from jax import lax
from jax.sharding import PartitionSpec as P

D = 768
HEADS = 12
HEAD = 64
FEAT = 128
STRETCH = 64
top_precision = lax.Precision.HIGHEST
norm_epsilon = 1e-05


def prefix(value, axis, combine, identity):
    count, here = (lax.axis_size(axis), lax.axis_index(axis))
    everything = jax.tree.map(
        lambda part, kind: lax.all_gather(part.astype(kind), axis),
        value,
        (jnp.bfloat16, jnp.bfloat16),
    )
    start = jax.tree.map(
        lambda part, zero: jnp.broadcast_to(jnp.asarray(zero, part.dtype), part.shape),
        value,
        identity,
    )

    def lap(k, before):
        reached = k < here
        new = combine(
            before, jax.tree.map(lambda part, own: part[k].astype(own.dtype), everything, value)
        )
        return jax.tree.map(lambda a, b: jnp.where(reached, a, b), new, before)

    return lax.fori_loop(0, count, lap, start)


def prefix_2(value, axis, join, neutral):
    count = lax.axis_size(axis)
    place = lax.axis_index(axis)
    ahead = count - 1 - place
    gathered = jax.tree.map(
        lambda a, kind: lax.all_gather(a.astype(kind), axis),
        value,
        jax.tree.map(lambda a: jnp.bfloat16 if a.dtype == jnp.float32 else a.dtype, value),
    )
    state = jax.tree.map(lambda a, e: jnp.zeros_like(a) + jnp.asarray(e, a.dtype), value, neutral)

    def one(lap, state):
        source = count - 1 - lap
        return join(
            state,
            jax.tree.map(
                lambda a, own: lax.dynamic_index_in_dim(a, source, 0, False).astype(own.dtype),
                gathered,
                value,
            ),
        )

    return lax.fori_loop(0, ahead, one, state)


def layer_norm(rows_in, gain, offset):
    centred = rows_in - jnp.mean(rows_in, axis=-1, keepdims=True)
    spread = jnp.mean(centred * centred, axis=-1, keepdims=True)
    return centred * lax.rsqrt(spread + norm_epsilon) * gain + offset


def featurize(inputs):
    return jnp.concatenate(
        [jax.nn.softmax(inputs, axis=-1), jax.nn.softmax(-inputs, axis=-1)], axis=-1
    )


def featurize_pair(u_query, u_key):
    return (featurize(u_query), featurize(u_key))


def gelu_tanh(pre_act):
    return jax.nn.gelu(pre_act, approximate=True)


def add_states(earlier, later):
    return jax.tree.map(jnp.add, earlier, later)


def shifted_sum(terms):
    running = jnp.cumsum(terms, axis=0)
    return jnp.concatenate([jnp.zeros_like(terms[:1]), running[:-1]], axis=0)


def attend_local(query_wide, key_wide, value_wide, prior_state, prior_total):
    length = query_wide.shape[0]
    blocks = length // STRETCH
    block_q = query_wide.reshape(blocks, STRETCH, HEADS, FEAT)
    block_k = key_wide.reshape(blocks, STRETCH, HEADS, FEAT)
    block_v = value_wide.reshape(blocks, STRETCH, HEADS, HEAD)
    state_terms = jnp.einsum("nshf,nshe->nhfe", block_k, block_v, precision=top_precision)
    total_terms = jnp.sum(block_k, axis=1)
    state_before = prior_state[None] + shifted_sum(state_terms)
    total_before = prior_total[None] + shifted_sum(total_terms)
    positions = jnp.arange(STRETCH)
    causal = positions[:, None] >= positions[None, :]
    scores = jnp.where(
        causal, jnp.einsum("nthf,nshf->nhts", block_q, block_k, precision=top_precision), 0.0
    )
    numerator = jnp.einsum("nhts,nshe->nthe", scores, block_v, precision=top_precision)
    numerator = numerator + jnp.einsum(
        "nthf,nhfe->nthe", block_q, state_before, precision=top_precision
    )
    denominator = jnp.transpose(jnp.sum(scores, axis=3), (0, 2, 1))
    denominator = denominator + jnp.einsum(
        "nthf,nhf->nth", block_q, total_before, precision=top_precision
    )
    return (numerator / denominator[..., None]).reshape(length, HEADS, HEAD)


def shards(
    tokens,
    gain_attn,
    bias_attn,
    w_qkv,
    w_feature,
    w_out,
    gain_mlp,
    bias_mlp,
    w_up,
    w_down,
    cotangent,
):
    shard_count = lax.axis_size("shard")
    local_weights = (
        gain_attn,
        bias_attn,
        w_qkv,
        w_feature,
        w_out,
        gain_mlp,
        bias_mlp,
        w_up,
        w_down,
    )
    totals = [
        jnp.zeros((weight.shape[0] * shard_count,) + weight.shape[1:], jnp.float32)
        for weight in local_weights
    ]
    results = []
    input_grads = []
    for batch_index in range(tokens.shape[0]):
        forward_set = (
            lax.all_gather(gain_attn, "shard", axis=0, tiled=True),
            lax.all_gather(bias_attn, "shard", axis=0, tiled=True),
            lax.all_gather(w_qkv, "shard", axis=0, tiled=True),
            lax.all_gather(w_feature, "shard", axis=0, tiled=True),
            lax.all_gather(w_out, "shard", axis=0, tiled=True),
            lax.all_gather(gain_mlp, "shard", axis=0, tiled=True),
            lax.all_gather(bias_mlp, "shard", axis=0, tiled=True),
            lax.all_gather(w_up, "shard", axis=0, tiled=True),
            lax.all_gather(w_down, "shard", axis=0, tiled=True),
        )
        (
            gain_one,
            bias_one,
            qkv_weight,
            feature_weight,
            out_weight,
            gain_two,
            bias_two,
            up_weight,
            down_weight,
        ) = forward_set
        rows_in = tokens[batch_index].astype(jnp.float32)
        length = rows_in.shape[0]
        normed, norm_pull = jax.vjp(
            layer_norm, rows_in, gain_one.astype(jnp.float32), bias_one.astype(jnp.float32)
        )
        normed_low = normed.astype(jnp.bfloat16)
        mixed = jnp.dot(normed_low, qkv_weight, preferred_element_type=jnp.float32).astype(
            jnp.bfloat16
        )
        queries = mixed[:, :D].reshape(length, HEADS, HEAD)
        key_rows = mixed[:, D : 2 * D].reshape(length, HEADS, HEAD)
        values = mixed[:, 2 * D :].reshape(length, HEADS, HEAD)
        feature_maps = feature_weight.reshape(HEADS, HEAD, 2, HEAD)
        u_query = jnp.einsum(
            "thi,hio->tho", queries, feature_maps[:, :, 0], preferred_element_type=jnp.float32
        )
        u_key = jnp.einsum(
            "thi,hio->tho", key_rows, feature_maps[:, :, 1], preferred_element_type=jnp.float32
        )
        (f_query, f_key), feature_pull = jax.vjp(featurize_pair, u_query, u_key)
        query_low = f_query.astype(jnp.bfloat16)
        key_low = f_key.astype(jnp.bfloat16)
        query_wide = query_low.astype(jnp.float32)
        key_wide = key_low.astype(jnp.float32)
        value_wide = values.astype(jnp.float32)
        key_state = jnp.einsum("shf,she->hfe", key_low, values, preferred_element_type=jnp.float32)
        key_sum = jnp.sum(key_wide, axis=0)
        prior = prefix(
            (key_state, key_sum),
            "shard",
            add_states,
            (jnp.zeros_like(key_state), jnp.zeros_like(key_sum)),
        )
        attended, attend_pull = jax.vjp(
            attend_local, query_wide, key_wide, value_wide, prior[0], prior[1]
        )
        attended_low = attended.reshape(length, D).astype(jnp.bfloat16)
        resid = rows_in + jnp.dot(attended_low, out_weight, preferred_element_type=jnp.float32)
        normed_two, norm_two_pull = jax.vjp(
            layer_norm, resid, gain_two.astype(jnp.float32), bias_two.astype(jnp.float32)
        )
        normed_two_low = normed_two.astype(jnp.bfloat16)
        pre_act = jnp.dot(normed_two_low, up_weight, preferred_element_type=jnp.float32)
        hidden, gelu_pull = jax.vjp(gelu_tanh, pre_act)
        hidden_low = hidden.astype(jnp.bfloat16)
        result = resid + jnp.dot(hidden_low, down_weight, preferred_element_type=jnp.float32)
        results.append(result.astype(jnp.bfloat16))
        qkv_back, feature_back, out_back, up_back, down_back = (
            lax.all_gather(w_qkv, "shard", axis=0, tiled=True),
            lax.all_gather(w_feature, "shard", axis=0, tiled=True),
            lax.all_gather(w_out, "shard", axis=0, tiled=True),
            lax.all_gather(w_up, "shard", axis=0, tiled=True),
            lax.all_gather(w_down, "shard", axis=0, tiled=True),
        )
        grad_out = cotangent[batch_index]
        d_down = jnp.dot(hidden_low.T, grad_out, preferred_element_type=jnp.float32)
        d_hidden = jnp.dot(grad_out, down_back.T, preferred_element_type=jnp.float32)
        (d_pre,) = gelu_pull(d_hidden)
        d_pre_low = d_pre.astype(jnp.bfloat16)
        d_up = jnp.dot(normed_two_low.T, d_pre_low, preferred_element_type=jnp.float32)
        d_normed_two = jnp.dot(d_pre_low, up_back.T, preferred_element_type=jnp.float32)
        d_resid_two, d_gain_two, d_bias_two = norm_two_pull(d_normed_two)
        d_resid = grad_out.astype(jnp.float32) + d_resid_two
        d_resid_low = d_resid.astype(jnp.bfloat16)
        d_out = jnp.dot(attended_low.T, d_resid_low, preferred_element_type=jnp.float32)
        d_attended = jnp.dot(d_resid_low, out_back.T, preferred_element_type=jnp.float32).reshape(
            length, HEADS, HEAD
        )
        d_query_f, d_key_f, d_value_f, local_state, local_sum = attend_pull(d_attended)
        later = prefix_2(
            (local_state, local_sum),
            "shard",
            add_states,
            (jnp.zeros_like(local_state), jnp.zeros_like(local_sum)),
        )
        d_key_f = (
            d_key_f
            + jnp.einsum("hfe,she->shf", later[0], value_wide, precision=top_precision)
            + later[1][None]
        )
        d_value_f = d_value_f + jnp.einsum(
            "hfe,shf->she", later[0], key_wide, precision=top_precision
        )
        d_u_query, d_u_key = feature_pull((d_query_f, d_key_f))
        d_uq_low = d_u_query.astype(jnp.bfloat16)
        d_uk_low = d_u_key.astype(jnp.bfloat16)
        back_maps = feature_back.reshape(HEADS, HEAD, 2, HEAD)
        d_queries = jnp.einsum(
            "tho,hio->thi", d_uq_low, back_maps[:, :, 0], preferred_element_type=jnp.float32
        )
        d_keys = jnp.einsum(
            "tho,hio->thi", d_uk_low, back_maps[:, :, 1], preferred_element_type=jnp.float32
        )
        query_map_grad = jnp.einsum(
            "thi,tho->hio", queries, d_uq_low, preferred_element_type=jnp.float32
        )
        key_map_grad = jnp.einsum(
            "thi,tho->hio", key_rows, d_uk_low, preferred_element_type=jnp.float32
        )
        d_maps = jnp.stack([query_map_grad, key_map_grad], axis=2).reshape(D, FEAT)
        d_mixed = jnp.concatenate(
            [d_queries.reshape(length, D), d_keys.reshape(length, D), d_value_f.reshape(length, D)],
            axis=1,
        ).astype(jnp.bfloat16)
        d_qkv = jnp.dot(normed_low.T, d_mixed, preferred_element_type=jnp.float32)
        d_normed = jnp.dot(d_mixed, qkv_back.T, preferred_element_type=jnp.float32)
        d_rows, d_gain_one, d_bias_one = norm_pull(d_normed)
        input_grads.append((d_resid + d_rows).astype(jnp.bfloat16))
        contributions = (
            d_gain_one,
            d_bias_one,
            d_qkv,
            d_maps,
            d_out,
            d_gain_two,
            d_bias_two,
            d_up,
            d_down,
        )
        totals = [total_sum + new_term for total_sum, new_term in zip(totals, contributions)]
    shares = (
        lax.psum_scatter(
            totals[0].astype(jnp.bfloat16), "shard", scatter_dimension=0, tiled=True
        ).astype(jnp.float32),
        lax.psum_scatter(
            totals[1].astype(jnp.bfloat16), "shard", scatter_dimension=0, tiled=True
        ).astype(jnp.float32),
        lax.psum_scatter(
            totals[2].astype(jnp.bfloat16), "shard", scatter_dimension=0, tiled=True
        ).astype(jnp.float32),
        lax.psum_scatter(
            totals[3].astype(jnp.bfloat16), "shard", scatter_dimension=0, tiled=True
        ).astype(jnp.float32),
        lax.psum_scatter(
            totals[4].astype(jnp.bfloat16), "shard", scatter_dimension=0, tiled=True
        ).astype(jnp.float32),
        lax.psum_scatter(
            totals[5].astype(jnp.bfloat16), "shard", scatter_dimension=0, tiled=True
        ).astype(jnp.float32),
        lax.psum_scatter(
            totals[6].astype(jnp.bfloat16), "shard", scatter_dimension=0, tiled=True
        ).astype(jnp.float32),
        lax.psum_scatter(
            totals[7].astype(jnp.bfloat16), "shard", scatter_dimension=0, tiled=True
        ).astype(jnp.float32),
        lax.psum_scatter(
            totals[8].astype(jnp.bfloat16), "shard", scatter_dimension=0, tiled=True
        ).astype(jnp.float32),
    )
    reduced = (
        lax.psum(shares[0].astype(jnp.bfloat16), "rep").astype(jnp.float32),
        lax.psum(shares[1].astype(jnp.bfloat16), "rep").astype(jnp.float32),
        lax.psum(shares[2].astype(jnp.bfloat16), "rep").astype(jnp.float32),
        lax.psum(shares[3].astype(jnp.bfloat16), "rep").astype(jnp.float32),
        lax.psum(shares[4].astype(jnp.bfloat16), "rep").astype(jnp.float32),
        lax.psum(shares[5].astype(jnp.bfloat16), "rep").astype(jnp.float32),
        lax.psum(shares[6].astype(jnp.bfloat16), "rep").astype(jnp.float32),
        lax.psum(shares[7].astype(jnp.bfloat16), "rep").astype(jnp.float32),
        lax.psum(shares[8].astype(jnp.bfloat16), "rep").astype(jnp.float32),
    )
    return (
        jnp.stack(results),
        jnp.stack(input_grads),
        reduced[0],
        reduced[1],
        reduced[2],
        reduced[3],
        reduced[4],
        reduced[5],
        reduced[6],
        reduced[7],
        reduced[8],
    )


def solution(mesh):
    placed = (
        P("rep", "shard", None),
        P("shard"),
        P("shard"),
        P("shard", None),
        P("shard", None),
        P("shard", None),
        P("shard"),
        P("shard"),
        P("shard", None),
        P("shard", None),
        P("rep", "shard", None),
    )
    return jax.shard_map(
        shards,
        mesh=mesh,
        in_specs=placed,
        out_specs=(
            P("rep", "shard", None),
            P("rep", "shard", None),
            P("shard"),
            P("shard"),
            P("shard", None),
            P("shard", None),
            P("shard", None),
            P("shard"),
            P("shard"),
            P("shard", None),
            P("shard", None),
        ),
        check_vma=False,
    )
```

profile of v0, /device:TPU:0, one launch (start us, length us, event | category | flops | bytes accessed | tf_op | source)
XLA Modules:
  0.0 919.0 jit_solution(16887876758495918346)
XLA Ops:
  14.7 14.5 %all-reduce.15 = (bf16[768]{0:T(1024)(128)(2,1)S(1)}, bf16[768]{0:T(1024)(128)(2,1)S(1)}, bf16[768]{0:T(1024)(128)(2,1)}, bf16[768]{0:T(1024)(128)(2,1)}) all-reduce(bf16[768]{0:T(1024)(128)(2,1)S(1)} %dynamic-update-slice.1, bf16[768]{0:T(1024)(128)(2,1)S(1)} %dynamic-update-slice, ...), channel_id=1, replica_groups=mesh['rep'=8,'shard'=4] {'shard'}, use_global_device_ids=true, to_apply=%add.5 | all-reduce | flops 3072 | bytes 12288
  30.4 14.9 %all_gather.89 = bf16[768,128]{1,0:T(8,128)(2,1)S(1)} all-gather(bf16[192,128]{1,0:T(8,128)(2,1)S(1)} %copy-done.179), channel_id=1, replica_groups=mesh['rep'=8,'shard'=4] {'shard'}, dimensions={0}, use_global_device_ids=true | all-gather | bytes 245760 | tf_op jit(solution)/shard_map/all_gather | solution.py:154
  51.4 34.1 %all-gather.17.cloned.1.call-done = bf16[768,2304]{1,0:T(8,128)(2,1)} async-done(((bf16[192,2304]{1,0:T(8,128)(2,1)}), bf16[768,2304]{1,0:T(8,128)(2,1)}) %all-gather.17.cloned.1.call-update) | async-done | bytes 3538960 | tf_op jit(solution)/shard_map/all_gather | solution.py:153
  159.9 30.2 %all-gather.2 = bf16[48,128,64]{1,2,0:T(8,128)(2,1)} all-gather(bf16[12,128,64]{1,2,0:T(8,128)(2,1)S(1)} %convolution_convert_fusion.6), channel_id=4, replica_groups=mesh['rep'=8,'shard'=4] {'shard'}, dimensions={0}, use_global_device_ids=true | all-gather | bytes 983040 | tf_op jit(solution)/shard_map/all_gather | solution.py:18
  190.1 13.3 %all-gather.9 = bf16[4,12,128]{2,1,0:T(8,128)(2,1)S(1)} all-gather(bf16[1,12,128]{2,1,0:T(8,128)(2,1)S(1)} %bitcast.581), channel_id=5, replica_groups=mesh['rep'=8,'shard'=4] {'shard'}, dimensions={0}, use_global_device_ids=true | all-gather | bytes 15360 | tf_op jit(solution)/shard_map/all_gather | solution.py:18
  203.4 6.6 while.63
  226.2 4.9 fusion.40
  249.9 30.3 %all-gather = bf16[48,128,64]{1,2,0:T(8,128)(2,1)} all-gather(bf16[12,128,64]{1,2,0:T(8,128)(2,1)S(1)} %convolution_convert_fusion.7), channel_id=2, replica_groups=mesh['rep'=8,'shard'=4] {'shard'}, dimensions={0}, use_global_device_ids=true | all-gather | bytes 983040 | tf_op jit(solution)/shard_map/all_gather | solution.py:18
  280.2 13.9 %all-gather.8 = bf16[4,12,128]{2,1,0:T(8,128)(2,1)S(1)} all-gather(bf16[1,12,128]{2,1,0:T(8,128)(2,1)S(1)} %bitcast.580), channel_id=3, replica_groups=mesh['rep'=8,'shard'=4] {'shard'}, dimensions={0}, use_global_device_ids=true | all-gather | bytes 15360 | tf_op jit(solution)/shard_map/all_gather | solution.py:18
  294.1 6.6 while.62
  332.0 5.6 fusion.215
  340.8 6.4 fusion.21
  400.3 19.6 %all-gather.6 = bf16[48,128,64]{1,2,0:T(8,128)(2,1)} all-gather(bf16[12,128,64]{1,2,0:T(8,128)(2,1)S(1)} %copy-done.148), channel_id=8, replica_groups=mesh['rep'=8,'shard'=4] {'shard'}, dimensions={0}, use_global_device_ids=true | all-gather | bytes 983040 | tf_op jit(solution)/shard_map/all_gather | solution.py:43
  419.9 13.1 %all-gather.11 = bf16[4,12,128]{2,1,0:T(8,128)(2,1)S(1)} all-gather(bf16[1,12,128]{2,1,0:T(8,128)(2,1)S(1)} %bitcast.583), channel_id=9, replica_groups=mesh['rep'=8,'shard'=4] {'shard'}, dimensions={0}, use_global_device_ids=true | all-gather | bytes 15360 | tf_op jit(solution)/shard_map/all_gather | solution.py:43
  474.4 16.5 %all-gather.4 = bf16[48,128,64]{1,2,0:T(8,128)(2,1)} all-gather(bf16[12,128,64]{1,2,0:T(8,128)(2,1)S(1)} %copy-done.147), channel_id=6, replica_groups=mesh['rep'=8,'shard'=4] {'shard'}, dimensions={0}, use_global_device_ids=true | all-gather | bytes 983040 | tf_op jit(solution)/shard_map/all_gather | solution.py:43
  490.9 13.1 %all-gather.10 = bf16[4,12,128]{2,1,0:T(8,128)(2,1)S(1)} all-gather(bf16[1,12,128]{2,1,0:T(8,128)(2,1)S(1)} %bitcast.582), channel_id=7, replica_groups=mesh['rep'=8,'shard'=4] {'shard'}, dimensions={0}, use_global_device_ids=true | all-gather | bytes 15360 | tf_op jit(solution)/shard_map/all_gather | solution.py:43
  599.4 5.2 fusion.78
  604.8 24.6 %reduce-scatter.6.cloned.1.call-done = bf16[192,2304]{1,0:T(8,128)(2,1)} async-done(((bf16[768,2304]{1,0:T(8,128)(2,1)}), bf16[192,2304]{1,0:T(8,128)(2,1)}) %reduce-scatter.6.cloned.1.call-update) | async-done | bytes 884752 | tf_op jit(solution)/shard_map/reduce_scatter | solution.py:299
  629.4 87.9 %reduce-scatter.12.cloned.1.call-done = bf16[192,3072]{1,0:T(8,128)(2,1)} async-done(((bf16[768,3072]{1,0:T(8,128)(2,1)}), bf16[192,3072]{1,0:T(8,128)(2,1)}) %reduce-scatter.12.cloned.1.call-update) | async-done | bytes 1179664 | tf_op jit(solution)/shard_map/reduce_scatter | solution.py:314
  717.2 88.1 %reduce-scatter.14.cloned.1.call-done = bf16[768,768]{1,0:T(8,128)(2,1)} async-done(((bf16[3072,768]{1,0:T(8,128)(2,1)}), bf16[768,768]{1,0:T(8,128)(2,1)}) %reduce-scatter.14.cloned.1.call-update) | async-done | bytes 1179664 | tf_op jit(solution)/shard_map/reduce_scatter | solution.py:317
  806.0 11.1 %all-reduce.14 = (bf16[768]{0:T(1024)(128)(2,1)S(1)}, bf16[768]{0:T(1024)(128)(2,1)S(1)}, bf16[768]{0:T(1024)(128)(2,1)S(1)}, bf16[768]{0:T(1024)(128)(2,1)S(1)}) all-reduce(bf16[768]{0:T(1024)(128)(2,1)S(1)} %copy-done.224, bf16[768]{0:T(1024)(128)(2,1)S(1)} %add_convert_fusion.14, ...), channel_id=10, replica_groups=mesh['rep'=8,'shard'=4] {'shard'}, use_global_device_ids=true, to_apply=%region_70.71.clone | all-reduce | flops 3072 | bytes 12288
  817.4 5.4 fusion.79
  828.2 24.5 %all-reduce.12 = (bf16[192]{0:T(256)(128)(2,1)S(1)}, bf16[192]{0:T(256)(128)(2,1)S(1)}, bf16[192,128]{1,0:T(8,128)(2,1)S(1)}, bf16[192]{0:T(256)(128)(2,1)S(1)}, bf16[192]{0:T(256)(128)(2,1)S(1)}) all-reduce(bf16[192]{0:T(256)(128)(2,1)S(1)} %dynamic-slice.5, ...), channel_id=1, replica_groups=mesh['rep'=8,'shard'=4] {'rep'}, use_global_device_ids=true, to_apply=%region_71.72 | all-reduce | flops 25344 | bytes 101376 | tf_op jit(solution)/shard_map/psum | solution.py:322
  855.6 49.7 %all-reduce.18.cloned.1.call-done = (bf16[192,2304]{1,0:T(8,128)(2,1)}, bf16[192,768]{1,0:T(8,128)(2,1)}, bf16[192,3072]{1,0:T(8,128)(2,1)}, bf16[768,768]{1,0:T(8,128)(2,1)}) async-done(((bf16[192,2304]{1,0:T(8,128)(2,1)}, bf16[192,768]{1,0:T(8,128)(2,1)}, bf16[192,3072]{1,0:T(8,128)(2,1)}, bf16[768,768]{1,0:T(8,128)(2,1)}), (bf16[192,2304]{1,0:T(8,128)(2,1)}, bf16[192,768]{1,0:T(8,128)(2,1)}, ...) | async-done | bytes 3538960 | tf_op jit(solution)/shard_map/psum | solution.py:324
  (828 shorter events, 381.6 us)
Async XLA Ops:
  7.2 78.3 %all-gather.17.cloned.1.call-start = ((), (), s32[]{:S(2)}) async-start(), calls=%async_computation.5 | async-start | bytes 4423680 | tf_op jit(solution)/shard_map/all_gather | solution.py:153
  7.9 313.2 %all-gather.19.cloned.1.call-start = ((), (), s32[]{:S(2)}) async-start(), calls=%async_computation.6 | async-start | bytes 1474560 | tf_op jit(solution)/shard_map/all_gather | solution.py:155
  8.7 323.3 %all-gather.21.cloned.1.call-start = ((), (), s32[]{:S(2)}) async-start(), calls=%async_computation.7 | async-start | bytes 5898240 | tf_op jit(solution)/shard_map/all_gather | solution.py:158
  9.5 20.9 %copy-start.179 = (bf16[192,128]{1,0:T(8,128)(2,1)S(1)}, bf16[192,128]{1,0:T(8,128)(2,1)}, u32[]{:S(2)}) copy-start(bf16[192,128]{1,0:T(8,128)(2,1)} %param.23) | copy-start | bytes 147460
  9.5 331.4 %all-gather.23.cloned.1.call-start = ((), (), s32[]{:S(2)}) async-start(), calls=%async_computation.8 | async-start | bytes 5898240 | tf_op jit(solution)/shard_map/all_gather | solution.py:159
  10.0 594.7 %reduce-scatter.10.cloned.1.call-start = ((), (), s32[]{:S(2)}) async-start(), calls=%async_computation.11 | async-start | bytes 1474560 | tf_op jit(solution)/shard_map/reduce_scatter | solution.py:305
  10.9 34.4 %copy-start.180 = (f32[256]{0:T(256)}, f32[256]{0:T(256)S(1)}, u32[]{:S(2)}) copy-start(f32[256]{0:T(256)S(1)} %get-tuple-element.658) | copy-start | bytes 3076
  10.9 34.4 %copy-start.188 = (f32[256]{0:T(256)}, f32[256]{0:T(256)S(1)}, u32[]{:S(2)}) copy-start(f32[256]{0:T(256)S(1)} %get-tuple-element.657) | copy-start | bytes 3076
  11.8 33.5 %copy-start.215 = (f32[256]{0:T(256)}, f32[256]{0:T(256)S(1)}, u32[]{:S(2)}) copy-start(f32[256]{0:T(256)S(1)} %get-tuple-element.512) | copy-start | bytes 3076
  47.2 45.6 %copy-start.72 = (bf16[12,64,1,64]{1,3,0,2:T(8,128)(2,1)}, bf16[12,64,1,64]{1,3,0,2:T(8,128)(2,1)S(1)}, u32[]{:S(2)}) copy-start(bf16[12,64,1,64]{1,3,0,2:T(8,128)(2,1)S(1)} %copy.272) | copy-start | bytes 294916
  47.5 51.9 %copy-start.75 = (bf16[12,64,1,64]{1,3,0,2:T(8,128)(2,1)}, bf16[12,64,1,64]{1,3,0,2:T(8,128)(2,1)S(1)}, u32[]{:S(2)}) copy-start(bf16[12,64,1,64]{1,3,0,2:T(8,128)(2,1)S(1)} %copy.273) | copy-start | bytes 294916
  102.9 56.7 %copy-start.63 = (bf16[256,12,64]{0,2,1:T(8,128)(2,1)}, bf16[256,12,64]{0,2,1:T(8,128)(2,1)S(1)}, u32[]{:S(2)}) copy-start(bf16[256,12,64]{0,2,1:T(8,128)(2,1)S(1)} %divide_convert_fusion) | copy-start | bytes 1179652
  158.3 31.8 %copy-start.83 = (bf16[256,768]{0,1:T(8,128)(2,1)}, bf16[256,768]{0,1:T(8,128)(2,1)S(1)}, u32[]{:S(2)}) copy-start(bf16[256,768]{0,1:T(8,128)(2,1)S(1)} %copy.174) | copy-start | bytes 1179652
  159.5 30.6 %copy-start.199 = (bf16[12,128]{1,0:T(8,128)(2,1)S(1)}, bf16[12,128]{1,0:T(8,128)(2,1)}, u32[]{:S(2)}) copy-start(bf16[12,128]{1,0:T(8,128)(2,1)} %fusion.139) | copy-start | bytes 9220
  248.2 32.0 %copy-start.81 = (bf16[256,768]{0,1:T(8,128)(2,1)}, bf16[256,768]{0,1:T(8,128)(2,1)S(1)}, u32[]{:S(2)}) copy-start(bf16[256,768]{0,1:T(8,128)(2,1)S(1)} %copy.157) | copy-start | bytes 1179652
  249.5 30.7 %copy-start.198 = (bf16[12,128]{1,0:T(8,128)(2,1)S(1)}, bf16[12,128]{1,0:T(8,128)(2,1)}, u32[]{:S(2)}) copy-start(bf16[12,128]{1,0:T(8,128)(2,1)} %fusion.140) | copy-start | bytes 9220
  302.6 11.5 %copy-start.2 = (bf16[4,64,12,128]{3,1,2,0:T(8,128)(2,1)}, bf16[4,64,12,128]{3,1,2,0:T(8,128)(2,1)S(1)}, u32[]{:S(2)}) copy-start(bf16[4,64,12,128]{3,1,2,0:T(8,128)(2,1)S(1)} %get-tuple-element.589) | copy-start | bytes 2359300
  323.3 34.7 %copy-start.11 = (f32[256,768]{1,0:T(8,128)}, f32[256,768]{1,0:T(8,128)S(1)}, u32[]{:S(2)}) copy-start(f32[256,768]{1,0:T(8,128)S(1)} %get-tuple-element.636) | copy-start | bytes 2359300
  470.6 20.4 %copy-start.200 = (bf16[12,128]{1,0:T(8,128)(2,1)S(1)}, bf16[12,128]{1,0:T(8,128)(2,1)}, u32[]{:S(2)}) copy-start(bf16[12,128]{1,0:T(8,128)(2,1)} %fusion.187) | copy-start | bytes 9220
  536.8 92.5 %reduce-scatter.6.cloned.1.call-start = ((), (), s32[]{:S(2)}) async-start(), calls=%async_computation.9 | async-start | bytes 4423680 | tf_op jit(solution)/shard_map/reduce_scatter | solution.py:299
  566.5 150.8 %reduce-scatter.12.cloned.1.call-start = ((), (), s32[]{:S(2)}) async-start(), calls=%async_computation.12 | async-start | bytes 5898240 | tf_op jit(solution)/shard_map/reduce_scatter | solution.py:314
  574.7 230.6 %reduce-scatter.14.cloned.1.call-start = ((), (), s32[]{:S(2)}) async-start(), calls=%async_computation.13 | async-start | bytes 5898240 | tf_op jit(solution)/shard_map/reduce_scatter | solution.py:317
  584.0 244.1 %reduce-scatter.8.cloned.1.call-start = ((), (), s32[]{:S(2)}) async-start(), calls=%async_computation.10 | async-start | bytes 245760 | tf_op jit(solution)/shard_map/reduce_scatter | solution.py:302
  599.2 306.1 %all-reduce.18.cloned.1.call-start = ((), (), s32[]{:S(2)}) async-start(), calls=%async_computation.14 | async-start | bytes 7077888 | tf_op jit(solution)/shard_map/psum | solution.py:324
  (231 other events, 687.1 us)
Sparse Core Ops, SparseCore 0:
  9.6 75.8 all-gather.16
  87.1 29.1 all-gather.18
  117.9 101.2 all-gather.20
  220.5 100.6 all-gather.22
  536.9 25.0 reduce-scatter.9
  566.5 62.7 reduce-scatter.5
  631.7 85.5 reduce-scatter.11
  719.5 85.7 reduce-scatter.13
  808.2 19.9 reduce-scatter.7
  832.1 73.0 all-reduce.17
where the time goes:
time: 925 us; the launch traced here: 919 us
  waiting for transfers between devices  289 us (31%)
  blocking collectives  215 us (23%)
  matrix products  169 us (18%)
  local copies, waits for them, and re-layouts  144 us (16%)
  other arithmetic  81.6 us (9%)
  between operations  18.6 us (2%)
    reduce_scatter x1, waiting for transfers between devices, shards(): lax.psum_scatter(totals[8].astype(jnp.bfloat16), 'shard', scatter_dimensi...  88.1 us
    reduce_scatter x1, waiting for transfers between devices, shards(): lax.psum_scatter(totals[7].astype(jnp.bfloat16), 'shard', scatter_dimensi...  87.9 us
    all_gather x4, blocking collectives, prefix(): lax.all_gather(part.astype(kind), axis)  87.6 us
    all_gather x4, blocking collectives, prefix_2(): lax.all_gather(a.astype(kind), axis)  62.3 us
    psum x1, waiting for transfers between devices, shards(): lax.psum(shares[2].astype(jnp.bfloat16), 'rep').astype(jnp.float32)  49.7 us
    all_gather x1, waiting for transfers between devices, shards(): lax.all_gather(w_qkv, 'shard', axis=0, tiled=True)  34.1 us
    unnamed x505, local copies, waits for them, and re-layouts  32.8 us
    concatenate x16, local copies, waits for them, and re-layouts, featurize(): jnp.concatenate([jax.nn.softmax(inputs, axis=-1), jax.nn.softmax(-inputs,...  32.5 us
  transfers between devices with their start and end apart: 10, of which 6 were waited for; matrix products, arithmetic and copies ran while one was open for 27% of the time, Pallas kernels for 0%

commit v1 on v0

--- a/solution.py
+++ b/solution.py
@@ -10,6 +10,19 @@
 STRETCH = 64
 top_precision = lax.Precision.HIGHEST
 norm_epsilon = 1e-05
+
+
+def gather_around(x, axis, dim):
+    size, index, span = (lax.axis_size(axis), lax.axis_index(axis), x.shape[dim])
+    right = [(i, (i + 1) % size) for i in range(size)]
+    whole = jnp.zeros((*x.shape[:dim], size * span, *x.shape[dim + 1 :]), x.dtype)
+    carried = x
+    for step in range(size):
+        holder = (index - step) % size
+        whole = lax.dynamic_update_slice_in_dim(whole, carried, holder * span, axis=dim)
+        if step < size - 1:
+            carried = lax.ppermute(carried, axis, right)
+    return whole
 
 
 def prefix(value, axis, combine, identity):
@@ -150,7 +163,7 @@
         forward_set = (
             lax.all_gather(gain_attn, "shard", axis=0, tiled=True),
             lax.all_gather(bias_attn, "shard", axis=0, tiled=True),
-            lax.all_gather(w_qkv, "shard", axis=0, tiled=True),
+            gather_around(w_qkv, "shard", 0),
             lax.all_gather(w_feature, "shard", axis=0, tiled=True),
             lax.all_gather(w_out, "shard", axis=0, tiled=True),
             lax.all_gather(gain_mlp, "shard", axis=0, tiled=True),

time: 925 us -> 1020 us (1.10)
  blocking collectives: 215 us -> 275 us
  other arithmetic: 81.6 us -> 92.1 us
    unnamed x2, blocking collectives: 25.6 us -> 69.8 us
    all_gather x1, blocking collectives: 14.9 us -> 53.3 us  [shards(): lax.all_gather(w_feature, 'shard', axis=0, tiled=True)]
    all_gather x1, waiting for transfers between devices: 34.1 us -> 0.01 us  [shards(): lax.all_gather(w_qkv, 'shard', axis=0, tiled=True)]
    ppermute x0 -> x3, waiting for transfers between devices: none -> 31.6 us  [gather_around(): carried = lax.ppermute(carried, axis, right)]
    all_gather x4, blocking collectives: 87.6 us -> 67.5 us  [prefix(): lax.all_gather(part.astype(kind), axis)]
    unnamed x505 -> x519, local copies, waits for them, and re-layouts: 32.8 us -> 34 us
  transfers between devices with their start and end apart: 10 -> 13, of which waited for: 6 -> 6; matrix products, arithmetic and copies ran while one was open for 27% -> 39% of each run, Pallas kernels for 0% -> 0%
where the time goes in v1:
time: 1020 us; the launch traced here: 1010 us
  waiting for transfers between devices  291 us (29%)
  blocking collectives  275 us (27%)
  matrix products  178 us (17%)
  local copies, waits for them, and re-layouts  149 us (15%)
  other arithmetic  92.1 us (9%)
  between operations  18.6 us (2%)
  starting transfers between devices  10.4 us (1%)
    reduce_scatter x1, waiting for transfers between devices, shards(): lax.psum_scatter(totals[8].astype(jnp.bfloat16), 'shard', scatter_dimensi...  88.1 us
    reduce_scatter x1, waiting for transfers between devices, shards(): lax.psum_scatter(totals[7].astype(jnp.bfloat16), 'shard', scatter_dimensi...  87.9 us
    unnamed x2, blocking collectives  69.8 us
    all_gather x4, blocking collectives, prefix(): lax.all_gather(part.astype(kind), axis)  67.5 us
    all_gather x4, blocking collectives, prefix_2(): lax.all_gather(a.astype(kind), axis)  59.4 us
    all_gather x1, blocking collectives, shards(): lax.all_gather(w_feature, 'shard', axis=0, tiled=True)  53.3 us
    psum x1, waiting for transfers between devices, shards(): lax.psum(shares[2].astype(jnp.bfloat16), 'rep').astype(jnp.float32)  49.7 us
    unnamed x519, local copies, waits for them, and re-layouts  34 us
  transfers between devices with their start and end apart: 13, of which 6 were waited for; matrix products, arithmetic and copies ran while one was open for 39% of the time, Pallas kernels for 0%

profile of v1, /device:TPU:0, one launch (start us, length us, event | category | flops | bytes accessed | tf_op | source)
XLA Modules:
  0.0 1013.9 jit_solution(5791942358656270327)
XLA Ops:
  13.3 31.6 %collective-permute-done = bf16[192,2304]{1,0:T(8,128)(2,1)S(1)} collective-permute-done((bf16[192,2304]{1,0:T(8,128)(2,1)S(1)}, bf16[192,2304]{1,0:T(8,128)(2,1)S(1)}, u32[]{:S(2)}, u32[]{:S(2)}) %collective-permute-start) | collective-permute-done | bytes 884768 | tf_op jit(solution)/shard_map/ppermute | solution.py:24
  44.9 6.3 collective-permute-start.1
  51.2 53.3 %all_gather.86 = bf16[768,128]{1,0:T(8,128)(2,1)S(1)} all-gather(bf16[192,128]{1,0:T(8,128)(2,1)S(1)} %copy-done.183), channel_id=1, replica_groups=mesh['rep'=8,'shard'=4] {'shard'}, dimensions={0}, use_global_device_ids=true | all-gather | bytes 245760 | tf_op jit(solution)/shard_map/all_gather | solution.py:167
  112.1 58.7 %all-reduce.15 = (bf16[768]{0:T(1024)(128)(2,1)S(1)}, bf16[768]{0:T(1024)(128)(2,1)S(1)}, bf16[768]{0:T(1024)(128)(2,1)}, bf16[768]{0:T(1024)(128)(2,1)}) all-reduce(bf16[768]{0:T(1024)(128)(2,1)S(1)} %dynamic-update-slice.1, bf16[768]{0:T(1024)(128)(2,1)S(1)} %dynamic-update-slice, ...), channel_id=1, replica_groups=mesh['rep'=8,'shard'=4] {'shard'}, use_global_device_ids=true, to_apply=%add.5 | all-reduce | flops 3072 | bytes 12288
  270.3 24.4 %all-gather.2 = bf16[48,128,64]{1,2,0:T(8,128)(2,1)} all-gather(bf16[12,128,64]{1,2,0:T(8,128)(2,1)S(1)} %convolution_convert_fusion.6), channel_id=4, replica_groups=mesh['rep'=8,'shard'=4] {'shard'}, dimensions={0}, use_global_device_ids=true | all-gather | bytes 983040 | tf_op jit(solution)/shard_map/all_gather | solution.py:31
  294.8 13.4 %all-gather.9 = bf16[4,12,128]{2,1,0:T(8,128)(2,1)S(1)} all-gather(bf16[1,12,128]{2,1,0:T(8,128)(2,1)S(1)} %bitcast.581), channel_id=5, replica_groups=mesh['rep'=8,'shard'=4] {'shard'}, dimensions={0}, use_global_device_ids=true | all-gather | bytes 15360 | tf_op jit(solution)/shard_map/all_gather | solution.py:31
  308.1 6.6 while.63
  358.4 16.4 %all-gather = bf16[48,128,64]{1,2,0:T(8,128)(2,1)} all-gather(bf16[12,128,64]{1,2,0:T(8,128)(2,1)S(1)} %convolution_convert_fusion.7), channel_id=2, replica_groups=mesh['rep'=8,'shard'=4] {'shard'}, dimensions={0}, use_global_device_ids=true | all-gather | bytes 983040 | tf_op jit(solution)/shard_map/all_gather | solution.py:31
  374.8 13.3 %all-gather.8 = bf16[4,12,128]{2,1,0:T(8,128)(2,1)S(1)} all-gather(bf16[1,12,128]{2,1,0:T(8,128)(2,1)S(1)} %bitcast.580), channel_id=3, replica_groups=mesh['rep'=8,'shard'=4] {'shard'}, dimensions={0}, use_global_device_ids=true | all-gather | bytes 15360 | tf_op jit(solution)/shard_map/all_gather | solution.py:31
  388.1 6.6 while.62
  422.4 5.6 fusion.215
  431.2 6.2 fusion.21
  477.2 16.5 %all-gather.6 = bf16[48,128,64]{1,2,0:T(8,128)(2,1)} all-gather(bf16[12,128,64]{1,2,0:T(8,128)(2,1)S(1)} %copy-done.153), channel_id=8, replica_groups=mesh['rep'=8,'shard'=4] {'shard'}, dimensions={0}, use_global_device_ids=true | all-gather | bytes 983040 | tf_op jit(solution)/shard_map/all_gather | solution.py:56
  493.7 13.4 %all-gather.11 = bf16[4,12,128]{2,1,0:T(8,128)(2,1)S(1)} all-gather(bf16[1,12,128]{2,1,0:T(8,128)(2,1)S(1)} %bitcast.583), channel_id=9, replica_groups=mesh['rep'=8,'shard'=4] {'shard'}, dimensions={0}, use_global_device_ids=true | all-gather | bytes 15360 | tf_op jit(solution)/shard_map/all_gather | solution.py:56
  539.1 16.4 %all-gather.4 = bf16[48,128,64]{1,2,0:T(8,128)(2,1)} all-gather(bf16[12,128,64]{1,2,0:T(8,128)(2,1)S(1)} %get-tuple-element.652), channel_id=6, replica_groups=mesh['rep'=8,'shard'=4] {'shard'}, dimensions={0}, use_global_device_ids=true | all-gather | bytes 983040 | tf_op jit(solution)/shard_map/all_gather | solution.py:56
  555.5 13.1 %all-gather.10 = bf16[4,12,128]{2,1,0:T(8,128)(2,1)S(1)} all-gather(bf16[1,12,128]{2,1,0:T(8,128)(2,1)S(1)} %bitcast.582), channel_id=7, replica_groups=mesh['rep'=8,'shard'=4] {'shard'}, dimensions={0}, use_global_device_ids=true | all-gather | bytes 15360 | tf_op jit(solution)/shard_map/all_gather | solution.py:56
  620.5 5.4 add_bitcast_fusion
  695.0 29.2 %reduce-scatter.6.cloned.1.call-done = bf16[192,2304]{1,0:T(8,128)(2,1)} async-done(((bf16[768,2304]{1,0:T(8,128)(2,1)}), bf16[192,2304]{1,0:T(8,128)(2,1)}) %reduce-scatter.6.cloned.1.call-update) | async-done | bytes 884752 | tf_op jit(solution)/shard_map/reduce_scatter | solution.py:312
  724.2 87.9 %reduce-scatter.12.cloned.1.call-done = bf16[192,3072]{1,0:T(8,128)(2,1)} async-done(((bf16[768,3072]{1,0:T(8,128)(2,1)}), bf16[192,3072]{1,0:T(8,128)(2,1)}) %reduce-scatter.12.cloned.1.call-update) | async-done | bytes 1179664 | tf_op jit(solution)/shard_map/reduce_scatter | solution.py:327
  812.1 88.1 %reduce-scatter.14.cloned.1.call-done = bf16[768,768]{1,0:T(8,128)(2,1)} async-done(((bf16[3072,768]{1,0:T(8,128)(2,1)}), bf16[768,768]{1,0:T(8,128)(2,1)}) %reduce-scatter.14.cloned.1.call-update) | async-done | bytes 1179664 | tf_op jit(solution)/shard_map/reduce_scatter | solution.py:330
  900.9 11.1 %all-reduce.14 = (bf16[768]{0:T(1024)(128)(2,1)S(1)}, bf16[768]{0:T(1024)(128)(2,1)S(1)}, bf16[768]{0:T(1024)(128)(2,1)S(1)}, bf16[768]{0:T(1024)(128)(2,1)S(1)}) all-reduce(bf16[768]{0:T(1024)(128)(2,1)S(1)} %copy-done.231, bf16[768]{0:T(1024)(128)(2,1)S(1)} %add_convert_fusion.14, ...), channel_id=10, replica_groups=mesh['rep'=8,'shard'=4] {'shard'}, use_global_device_ids=true, to_apply=%region_70.71.clone | all-reduce | flops 3072 | bytes 12288
  912.3 5.4 fusion.79
  923.0 24.6 %all-reduce.12 = (bf16[192]{0:T(256)(128)(2,1)S(1)}, bf16[192]{0:T(256)(128)(2,1)S(1)}, bf16[192,128]{1,0:T(8,128)(2,1)S(1)}, bf16[192]{0:T(256)(128)(2,1)S(1)}, bf16[192]{0:T(256)(128)(2,1)S(1)}) all-reduce(bf16[192]{0:T(256)(128)(2,1)S(1)} %dynamic-slice.5, ...), channel_id=1, replica_groups=mesh['rep'=8,'shard'=4] {'rep'}, use_global_device_ids=true, to_apply=%region_71.72 | all-reduce | flops 25344 | bytes 101376 | tf_op jit(solution)/shard_map/psum | solution.py:335
  950.5 49.7 %all-reduce.18.cloned.1.call-done = (bf16[192,2304]{1,0:T(8,128)(2,1)}, bf16[192,768]{1,0:T(8,128)(2,1)}, bf16[192,3072]{1,0:T(8,128)(2,1)}, bf16[768,768]{1,0:T(8,128)(2,1)}) async-done(((bf16[192,2304]{1,0:T(8,128)(2,1)}, bf16[192,768]{1,0:T(8,128)(2,1)}, bf16[192,3072]{1,0:T(8,128)(2,1)}, bf16[768,768]{1,0:T(8,128)(2,1)}), (bf16[192,2304]{1,0:T(8,128)(2,1)}, bf16[192,768]{1,0:T(8,128)(2,1)}, ...) | async-done | bytes 3538960 | tf_op jit(solution)/shard_map/psum | solution.py:337
  (853 shorter events, 413.3 us)
Async XLA Ops:
  7.2 328.9 %all-gather.17.cloned.1.call-start = ((), (), s32[]{:S(2)}) async-start(), calls=%async_computation.5 | async-start | bytes 1474560 | tf_op jit(solution)/shard_map/all_gather | solution.py:168
  7.9 414.4 %all-gather.19.cloned.1.call-start = ((), (), s32[]{:S(2)}) async-start(), calls=%async_computation.6 | async-start | bytes 5898240 | tf_op jit(solution)/shard_map/all_gather | solution.py:171
  8.7 42.5 %copy-start.183 = (bf16[192,128]{1,0:T(8,128)(2,1)S(1)}, bf16[192,128]{1,0:T(8,128)(2,1)}, u32[]{:S(2)}) copy-start(bf16[192,128]{1,0:T(8,128)(2,1)} %param.23) | copy-start | bytes 147460
  8.7 422.5 %all-gather.21.cloned.1.call-start = ((), (), s32[]{:S(2)}) async-start(), calls=%async_computation.7 | async-start | bytes 5898240 | tf_op jit(solution)/shard_map/all_gather | solution.py:172
  9.4 672.3 %all-gather.23.cloned.1.call-start = ((), (), s32[]{:S(2)}) async-start(), calls=%async_computation.8 | async-start | bytes 4423680 | tf_op jit(solution)/shard_map/all_gather | solution.py:233
  9.5 35.4 %collective-permute-start = (bf16[192,2304]{1,0:T(8,128)(2,1)S(1)}, bf16[192,2304]{1,0:T(8,128)(2,1)S(1)}, u32[]{:S(2)}, u32[]{:S(2)}) collective-permute-start(bf16[192,2304]{1,0:T(8,128)(2,1)S(1)} %copy-done.84), channel_id=1, source_target_pairs={{0,1},{1,2},{2,3},{3,0},{4,5},{5,6},{6,7},{7,4},{8,9},{9,10},{10,1... | collective-permute-start | bytes 2654216 | tf_op jit(solution)/shard_map/ppermute | solution.py:24
  12.6 682.4 %reduce-scatter.10.cloned.1.call-start = ((), (), s32[]{:S(2)}) async-start(), calls=%async_computation.11 | async-start | bytes 1474560 | tf_op jit(solution)/shard_map/reduce_scatter | solution.py:318
  12.9 91.8 %copy-start.184 = (f32[256]{0:T(256)}, f32[256]{0:T(256)S(1)}, u32[]{:S(2)}) copy-start(f32[256]{0:T(256)S(1)} %get-tuple-element.658) | copy-start | bytes 3076
  12.9 91.8 %copy-start.193 = (f32[256]{0:T(256)}, f32[256]{0:T(256)S(1)}, u32[]{:S(2)}) copy-start(f32[256]{0:T(256)S(1)} %get-tuple-element.657) | copy-start | bytes 3076
  13.2 91.4 %copy-start.221 = (f32[256]{0:T(256)}, f32[256]{0:T(256)S(1)}, u32[]{:S(2)}) copy-start(f32[256]{0:T(256)S(1)} %get-tuple-element.512) | copy-start | bytes 3076
  13.2 96.0 %copy-start.223 = (f32[256]{0:T(256)}, f32[256]{0:T(256)S(1)}, u32[]{:S(2)}) copy-start(f32[256]{0:T(256)S(1)} %get-tuple-element.511) | copy-start | bytes 3076
  44.9 61.4 %copy-start.136 = (bf16[192,2304]{1,0:T(8,128)(2,1)}, bf16[192,2304]{1,0:T(8,128)(2,1)S(1)}, u32[]{:S(2)}) copy-start(bf16[192,2304]{1,0:T(8,128)(2,1)S(1)} %collective-permute-done) | copy-start | bytes 2654212
  44.9 64.3 %collective-permute-start.1 = (bf16[192,2304]{1,0:T(8,128)(2,1)S(1)}, bf16[192,2304]{1,0:T(8,128)(2,1)}, u32[]{:S(2)}, u32[]{:S(2)}) collective-permute-start(bf16[192,2304]{1,0:T(8,128)(2,1)S(1)} %collective-permute-done), channel_id=1, source_target_pairs={{0,1},{1,2},{2,3},{3,0},{4,5},{5,6},{6,7},{7,4},{8,9},{9,10},{10,1... | collective-permute-start | bytes 2654216 | tf_op jit(solution)/shard_map/ppermute | solution.py:24
  109.2 71.0 %collective-permute-start.2 = (bf16[192,2304]{1,0:T(8,128)(2,1)}, bf16[192,2304]{1,0:T(8,128)(2,1)}, u32[]{:S(2)}, u32[]{:S(2)}) collective-permute-start(bf16[192,2304]{1,0:T(8,128)(2,1)} %collective-permute-done.1), channel_id=1, source_target_pairs={{0,1},{1,2},{2,3},{3,0},{4,5},{5,6},{6,7},{7,4},{8,9},{9,10},{10,1... | collective-permute-start | bytes 2654216 | tf_op jit(solution)/shard_map/ppermute | solution.py:24
  172.6 24.2 %copy-start.79 = (bf16[12,64,1,64]{1,3,0,2:T(8,128)(2,1)}, bf16[12,64,1,64]{1,3,0,2:T(8,128)(2,1)S(1)}, u32[]{:S(2)}) copy-start(bf16[12,64,1,64]{1,3,0,2:T(8,128)(2,1)S(1)} %copy.273) | copy-start | bytes 294916
  191.7 62.3 %copy-start.18 = (f32[256,12,64]{0,2,1:T(8,128)}, f32[256,12,64]{0,2,1:T(8,128)S(1)}, u32[]{:S(2)}) copy-start(f32[256,12,64]{0,2,1:T(8,128)S(1)} %get-tuple-element.626) | copy-start | bytes 2359300
  200.8 69.1 %copy-start.68 = (bf16[256,12,64]{0,2,1:T(8,128)(2,1)}, bf16[256,12,64]{0,2,1:T(8,128)(2,1)S(1)}, u32[]{:S(2)}) copy-start(bf16[256,12,64]{0,2,1:T(8,128)(2,1)S(1)} %divide_convert_fusion) | copy-start | bytes 1179652
  268.7 26.0 %copy-start.86 = (bf16[256,768]{0,1:T(8,128)(2,1)}, bf16[256,768]{0,1:T(8,128)(2,1)S(1)}, u32[]{:S(2)}) copy-start(bf16[256,768]{0,1:T(8,128)(2,1)S(1)} %copy.174) | copy-start | bytes 1179652
  269.9 24.8 %copy-start.206 = (bf16[12,128]{1,0:T(8,128)(2,1)S(1)}, bf16[12,128]{1,0:T(8,128)(2,1)}, u32[]{:S(2)}) copy-start(bf16[12,128]{1,0:T(8,128)(2,1)} %fusion.139) | copy-start | bytes 9220
  629.8 94.5 %reduce-scatter.6.cloned.1.call-start = ((), (), s32[]{:S(2)}) async-start(), calls=%async_computation.9 | async-start | bytes 4423680 | tf_op jit(solution)/shard_map/reduce_scatter | solution.py:312
  657.0 155.1 %reduce-scatter.12.cloned.1.call-start = ((), (), s32[]{:S(2)}) async-start(), calls=%async_computation.12 | async-start | bytes 5898240 | tf_op jit(solution)/shard_map/reduce_scatter | solution.py:327
  665.1 235.1 %reduce-scatter.14.cloned.1.call-start = ((), (), s32[]{:S(2)}) async-start(), calls=%async_computation.13 | async-start | bytes 5898240 | tf_op jit(solution)/shard_map/reduce_scatter | solution.py:330
  674.4 248.6 %reduce-scatter.8.cloned.1.call-start = ((), (), s32[]{:S(2)}) async-start(), calls=%async_computation.10 | async-start | bytes 245760 | tf_op jit(solution)/shard_map/reduce_scatter | solution.py:315
  689.3 310.8 %all-reduce.18.cloned.1.call-start = ((), (), s32[]{:S(2)}) async-start(), calls=%async_computation.14 | async-start | bytes 7077888 | tf_op jit(solution)/shard_map/psum | solution.py:337
  (241 other events, 738.1 us)
Sparse Core Ops, SparseCore 0:
  9.6 43.9 all-gather.16
  55.2 117.4 all-gather.18
  174.2 90.6 all-gather.20
  266.3 75.3 all-gather.22
  629.9 27.0 reduce-scatter.9
  659.1 65.0 reduce-scatter.5
  726.5 85.5 reduce-scatter.11
  814.4 85.7 reduce-scatter.13
  903.0 19.8 reduce-scatter.7
  926.9 73.1 all-reduce.17
